TPU v7x, 32 devices: a whole 2x2x4 slice. The times are simulated.
32 devices in a mesh: groups: 2 (over y), rows: 4 (over x, core), cols: 4 (over z).
Axes of the slice: x: 2, y: 2, z: 4, core: 2. Of those that a mesh axis runs over, the one named last changes fastest.
Arguments:
- pair_rep: float32 [384, 192, 128], P(('groups', 'cols'), 'rows'), parts along dimension 0, may hold values from -6 to 6
- token_mask: int32 [384], P(('groups', 'rows')), parts along dimension 0, may hold values from 0 to 1, as said below
- norm_gain: float32 [128], replicated, may hold values from 0.1 to 1.9
- norm_shift: float32 [128], replicated, may hold values from -3 to 3
- w_query: bfloat16 [128, 128], replicated, may hold values from -0.5 to 0.5
- w_keyval: bfloat16 [128, 256], replicated, may hold values from -0.5 to 0.5
- w_gate: bfloat16 [128, 128], replicated, may hold values from -0.5 to 0.5
- gate_shift: float32 [128], replicated, may hold values from -3 to 3
- w_bias: float32 [128, 4], replicated, may hold values from -12 to 12
- w_out: bfloat16 [128, 128], replicated, may hold values from -0.5 to 0.5
- out_shift: float32 [128], replicated, may hold values from -3 to 3
Outputs:
- pair_update: float32 [384, 192, 128], P(('groups', 'cols'), 'rows'), parts along dimension 0
There are 2 independent parts, one for each index of `groups`. A program takes and returns all parts, laid end to end along the dimension named above; an argument that names none is the same for every part. Nothing has to cross between parts.
Inputs may be any that keep to these rules, and one draw needn't show every extreme that they name: `token_mask`: position 0 is always a valid residue and the last position never is.
All inputs are finite; a program needn't handle non-finite values.
Results may differ from a plain program's by a relative error of at most 0.012.
The roundings to bfloat16 on the way count: a program that leaves them out, or rounds other values in their place, can miss the bound.
Values may be sent and summed in bfloat16 or wider, within the bound.
No kernel may reach another device: no remote copies, remote signals or barrier semaphores. Data moves between devices by JAX's collectives and lax.ppermute only.
A program may use at most 128 MiB of HBM per device.

v0:
```python
import jax
import jax.numpy as jnp
from jax import lax
from jax.sharding import PartitionSpec as P

HEADS = 4
HEAD_DIM = 32


def layer_norm(values, norm_gain, norm_shift):
    mean_val = jnp.mean(values, axis=-1, keepdims=True)
    centred = values - mean_val
    variance = jnp.mean(centred * centred, axis=-1, keepdims=True)
    return (centred * lax.rsqrt(variance + 1e-05) * norm_gain + norm_shift).astype(jnp.bfloat16)


def largest_divisor(count, limit):
    return max(
        (candidate for candidate in range(1, min(count, limit) + 1) if count % candidate == 0)
    )


def whole_row_layer(
    normed, token_mask, w_query, w_keyval, w_gate, gate_shift, w_bias, w_out, out_shift
):
    width = normed.shape[2]
    local_bias = jnp.dot(
        normed.astype(jnp.float32), w_bias, precision=lax.Precision.HIGHEST
    ).transpose(2, 0, 1)
    wide = lax.all_to_all(normed, "rows", split_axis=0, concat_axis=1, tiled=True)
    few_rows, token_count, _ = wide.shape
    bias_part = lax.all_gather(local_bias, "cols", axis=1, tiled=True)
    full_bias, full_mask = (
        lax.all_gather(bias_part, "rows", axis=2, tiled=True),
        lax.all_gather(token_mask.astype(jnp.float32), "rows", axis=0, tiled=True),
    )
    queries = (
        jnp.dot(wide, w_query, preferred_element_type=jnp.float32) * HEAD_DIM ** (-0.5)
    ).astype(jnp.bfloat16)
    queries = queries.reshape(few_rows, token_count, HEADS, HEAD_DIM)
    keyvals = jnp.dot(wide, w_keyval, preferred_element_type=jnp.float32).astype(jnp.bfloat16)
    keys = keyvals[..., :width].reshape(few_rows, token_count, HEADS, HEAD_DIM)
    values = keyvals[..., width:].reshape(few_rows, token_count, HEADS, HEAD_DIM)
    gates = jax.nn.sigmoid(jnp.dot(wide, w_gate, preferred_element_type=jnp.float32) + gate_shift)
    usable = full_mask > 0.5
    block_len = largest_divisor(token_count, 128)

    def one_block(block_index, gated_all):
        start = block_index * block_len
        query_block = lax.dynamic_slice_in_dim(queries, start, block_len, 1)
        bias_block = lax.dynamic_slice_in_dim(full_bias, start, block_len, 1)
        gate_block = lax.dynamic_slice_in_dim(gates, start, block_len, 1)
        scores = jnp.einsum(
            "ijhd,ikhd->hijk", query_block, keys, preferred_element_type=jnp.float32
        )
        scores = scores + bias_block[:, None]
        scores = jnp.where(usable[None, None, None, :], scores, jnp.float32(-1000000000.0))
        highest = jnp.max(scores, axis=-1, keepdims=True)
        expo = jnp.exp(scores - highest)
        total = jnp.sum(expo, axis=-1)
        weights = expo.astype(jnp.bfloat16)
        mixed = jnp.einsum("hijk,ikhd->ijhd", weights, values, preferred_element_type=jnp.float32)
        attended = mixed / total.transpose(1, 2, 0)[..., None]
        gated = (gate_block * attended.reshape(few_rows, block_len, width)).astype(jnp.bfloat16)
        return lax.dynamic_update_slice_in_dim(gated_all, gated, start, 1)

    gated_all = lax.fori_loop(
        0,
        token_count // block_len,
        one_block,
        jnp.zeros((few_rows, token_count, width), jnp.bfloat16),
    )
    gated_home = lax.all_to_all(gated_all, "rows", split_axis=1, concat_axis=0, tiled=True)
    return jnp.dot(gated_home, w_out, preferred_element_type=jnp.float32) + out_shift


def on_device(
    pair_rep,
    token_mask,
    norm_gain,
    norm_shift,
    w_query,
    w_keyval,
    w_gate,
    gate_shift,
    w_bias,
    w_out,
    out_shift,
):
    normed = layer_norm(pair_rep, norm_gain, norm_shift)
    return whole_row_layer(
        normed, token_mask, w_query, w_keyval, w_gate, gate_shift, w_bias, w_out, out_shift
    )


def solution(mesh):
    return jax.shard_map(
        on_device,
        mesh=mesh,
        in_specs=(
            P(("groups", "cols"), "rows", None),
            P(("groups", "rows")),
            P(),
            P(),
            P(),
            P(),
            P(),
            P(),
            P(),
            P(),
            P(),
        ),
        out_specs=P(("groups", "cols"), "rows", None),
        check_vma=False,
    )
```

profile of v0, /device:TPU:0, one launch (start us, length us, event | category | flops | bytes accessed | tf_op | source)
XLA Modules:
  0.0 85.9 jit_solution(3610924705760710887)
XLA Ops:
  0.0 1.7 %reduce_sum.31 = f32[48,48]{1,0:T(8,128)S(1)} reduce(f32[48,48,128]{2,1,0:T(8,128)} %param.13, f32[]{:T(128)} %constant.58.clone.1), dimensions={2}, to_apply=%region_0.0 | reduce | flops 292608 | bytes 1188868 | tf_op jit(solution)/shard_map/reduce_sum | solution.py:11
  1.8 0.7 multiply_reduce_fusion
  2.5 0.0 copy-start.7
  2.5 1.5 %add_convert_fusion = bf16[48,48,128]{2,1,0:T(8,128)(2,1)} fusion(f32[48,48,128]{2,1,0:T(8,128)S(1)} %copy-done.1, f32[128]{0:T(128)S(1)} %copy-done.8, f32[128]{0:T(128)S(1)} %copy-done.9, f32[48,48]{1,0:T(8,128)S(1)} %add_rsqrt_fusion, f32[48,48]{1,0:T(8,128)S(1)} %broadcast_multiply_fusion), kind=kLoop, calls=%fused_computation.31 | loop fusion | flops 1474560 | bytes 1788928 | tf_op jit(solution)/shard_map/convert_element_type | solution.py:14
  4.0 4.2 %all-to-all-start = ((bf16[48,48,128]{2,1,0:T(8,128)(2,1)}), bf16[48,48,128]{2,1,0:T(8,128)(2,1)S(1)}, u32[]{:S(2)}, u32[]{:S(2)}) async-start(bf16[48,48,128]{2,1,0:T(8,128)(2,1)} %add_convert_fusion), calls=%async_computation | async-start | bytes 1179648 | tf_op jit(solution)/shard_map/all_to_all | solution.py:30
  8.3 2.8 %convolution_bitcast_fusion = f32[4,48,48]{2,0,1:T(4,128)S(1)} fusion(bf16[48,48,128]{2,1,0:T(8,128)(2,1)} %add_convert_fusion, f32[128,4]{0,1:T(4,128)S(1)} %copy-done.7), kind=kOutput, calls=%fused_computation.33 | convolution fusion | flops 14155776 | bytes 628736 | tf_op jit(solution)/shard_map/dot_general | solution.py:27
  11.1 15.8 %all_gather.10 = f32[4,192,48]{2,0,1:T(4,128)S(1)} all-gather(f32[4,48,48]{2,0,1:T(4,128)S(1)} %convolution_bitcast_fusion), channel_id=1, replica_groups=mesh['groups'=2,'rows'=4,'cols'=4] {'cols'}, dimensions={1}, use_global_device_ids=true | all-gather | bytes 184320 | tf_op jit(solution)/shard_map/all_gather | solution.py:32
  27.0 0.2 copy.36
  27.2 0.6 dynamic-slice
  28.3 0.1 convert_dynamic-update-slice_fusion
  28.4 5.6 %all-reduce = f32[192]{0:T(256)S(1)} all-reduce(f32[192]{0:T(256)S(1)} %convert_dynamic-update-slice_fusion), channel_id=1, replica_groups=mesh['groups'=2,'rows'=4,'cols'=4] {'rows'}, use_global_device_ids=true, to_apply=%add | all-reduce | flops 192 | bytes 1536
  34.1 9.0 %all_gather.11 = f32[4,192,192]{1,0,2:T(4,128)S(1)} all-gather(f32[4,192,48]{1,0,2:T(4,128)S(1)} %copy.36), channel_id=1, replica_groups=mesh['groups'=2,'rows'=4,'cols'=4] {'rows'}, dimensions={2}, use_global_device_ids=true | all-gather | bytes 737280 | tf_op jit(solution)/shard_map/all_gather | solution.py:34
  43.1 0.0 all-to-all-done
  43.1 0.1 copy.33
  43.2 0.4 convolution_convert_fusion
  43.7 0.3 fusion.39
  44.0 0.3 copy.35
  44.3 0.0 copy-start.6
  44.3 0.9 %copy.40 = bf16[12,192,4,32]{1,3,0,2:T(8,128)(2,1)} copy(bf16[12,192,4,32]{1,3,2,0:T(8,128)(2,1)S(1)} %bitcast.59) | data formatting | bytes 1179648 | tf_op jit(solution)/shard_map/while | solution.py:67
  45.2 1.2 %copy.37 = bf16[12,192,128]{1,2,0:T(8,128)(2,1)} copy(bf16[12,192,128]{2,1,0:T(8,128)(2,1)S(1)} %get-tuple-element.188) | data formatting | bytes 1179648 | tf_op jit(solution)/shard_map/slice | solution.py:43
  46.4 0.3 fusion.28
  46.7 1.2 %copy.34 = bf16[12,192,128]{1,2,0:T(8,128)(2,1)} copy(bf16[12,192,128]{2,1,0:T(8,128)(2,1)S(1)} %fusion.28) | data formatting | bytes 1179648 | tf_op jit(solution)/shard_map/convert_element_type | solution.py:39
  47.9 1.5 %fusion.27 = f32[12,192,128]{2,1,0:T(8,128)} fusion(bf16[12,192,128]{2,1,0:T(8,128)(2,1)S(1)} %bitcast.58, f32[128]{0:T(128)S(1)} %copy-done.13, bf16[128,128]{1,0:T(8,128)(2,1)S(1)} %copy-done.11), kind=kOutput, calls=%fused_computation.29 | convolution fusion | flops 76677120 | bytes 1802752 | tf_op jit(solution)/shard_map/dot_general | solution.py:44
  49.3 1.0 %broadcast_in_dim.45.clone = bf16[12,192,128]{2,0,1:T(8,128)(2,1)} broadcast(bf16[]{:T(256)} %constant.57.clone.1), dimensions={} | broadcast | bytes 589826 | tf_op jit(solution)/shard_map/broadcast_in_dim | solution.py:71
  50.3 18.9 %while.13 = (s32[]{:T(128)}, bf16[12,192,128]{2,0,1:T(8,128)(2,1)}, f32[12,192,128]{2,1,0:T(8,128)}, pred[192]{0:T(512)(128)(4,1)S(1)}, bf16[12,192,4,32]{1,3,2,...) while((s32[]{:T(128)}, bf16[12,192,128]{2,0,1:T(8,128)(2,1)}, ...), condition=%wide.region_5.6_spmd, body=%wide.region_2.5_spmd.sunk | while | flops 118112448 | bytes 19440052 | solution.py:67
  50.3 0.3 constant_dynamic-slice_fusion.13
  50.6 0.2 copy.78
  50.8 4.4 %fusion.59 = (f32[4,12,96]{2,1,0:T(8,128)S(1)}, bf16[4,12,96,192]{3,2,1,0:T(8,128)(2,1)}) fusion(f32[4,96,192]{2,1,0:T(8,128)S(1)} %copy.78, pred[192]{0:T(512)(128)(4,1)S(1)} %get-tuple-element.270, bf16[12,192,4,32]{1,3,0,2:T(8,128)(2,1)S(1)} %get-tuple-element.272, bf16[12,192,4,32]{1,3,2,0:T(8,128)(2,1)} %get-tuple-element.271, s32[]{:T(128)S(6)} %select_n.31), kind=kOutput, calls=%fused_computation.43.clone.1 | convolution fusion | flops 61046976 | bytes 3066052 | tf_op jit(solution)/shard_map/while/body/eval_jaxpr/sub | solution.py:59
  55.3 0.0 copy-start.2
  55.3 2.9 %fusion.60 = f32[12,96,4,32]{1,3,2,0:T(8,128)S(1)} fusion(bf16[12,192,4,32]{1,3,2,0:T(8,128)(2,1)} %get-tuple-element.274, bf16[4,12,96,192]{3,2,1,0:T(8,128)(2,1)} %get-tuple-element.241, f32[12,96,4]{1,2,0:T(4,128)S(1)} %copy.79), kind=kOutput, calls=%fused_computation.10.clone.1 | convolution fusion | flops 56770560 | bytes 2967552 | tf_op jit(solution)/shard_map/while/body/eval_jaxpr/hijk,ikhd->ijhd/dot_general | solution.py:62
  58.2 0.1 constant_dynamic-slice_fusion.12
  58.3 0.3 copy.77
  58.5 0.1 fusion.61
  58.6 0.3 copy.80
  59.0 0.8 constant_dynamic-update-slice_fusion.2
  59.8 0.3 constant_dynamic-slice_fusion.13
  60.1 0.2 copy.78
  60.3 4.4 %fusion.59 = (f32[4,12,96]{2,1,0:T(8,128)S(1)}, bf16[4,12,96,192]{3,2,1,0:T(8,128)(2,1)}) fusion(f32[4,96,192]{2,1,0:T(8,128)S(1)} %copy.78, pred[192]{0:T(512)(128)(4,1)S(1)} %get-tuple-element.270, bf16[12,192,4,32]{1,3,0,2:T(8,128)(2,1)S(1)} %get-tuple-element.272, bf16[12,192,4,32]{1,3,2,0:T(8,128)(2,1)} %get-tuple-element.271, s32[]{:T(128)S(6)} %select_n.31), kind=kOutput, calls=%fused_computation.43.clone.1 | convolution fusion | flops 61046976 | bytes 3066052 | tf_op jit(solution)/shard_map/while/body/eval_jaxpr/sub | solution.py:59
  64.7 0.0 copy-start.2
  64.7 2.9 %fusion.60 = f32[12,96,4,32]{1,3,2,0:T(8,128)S(1)} fusion(bf16[12,192,4,32]{1,3,2,0:T(8,128)(2,1)} %get-tuple-element.274, bf16[4,12,96,192]{3,2,1,0:T(8,128)(2,1)} %get-tuple-element.241, f32[12,96,4]{1,2,0:T(4,128)S(1)} %copy.79), kind=kOutput, calls=%fused_computation.10.clone.1 | convolution fusion | flops 56770560 | bytes 2967552 | tf_op jit(solution)/shard_map/while/body/eval_jaxpr/hijk,ikhd->ijhd/dot_general | solution.py:62
  67.6 0.1 constant_dynamic-slice_fusion.12
  67.7 0.3 copy.77
  68.0 0.1 fusion.61
  68.1 0.3 copy.80
  68.4 0.8 constant_dynamic-update-slice_fusion.2
  69.2 15.2 %all_to_all.36 = bf16[12,192,128]{2,0,1:T(8,128)(2,1)S(1)} all-to-all(bf16[12,192,128]{2,0,1:T(8,128)(2,1)} %get-tuple-element.281), channel_id=1, replica_groups=mesh['groups'=2,'rows'=4,'cols'=4] {'rows'}, dimensions={1} | all-to-all | bytes 1179648 | tf_op jit(solution)/shard_map/all_to_all | solution.py:73
  84.4 0.2 copy.44
  84.6 1.3 %convolution_add_fusion = f32[48,48,128]{2,1,0:T(8,128)} fusion(bf16[48,48,128]{2,1,0:T(8,128)(2,1)S(1)} %bitcast.62, f32[128]{0:T(128)S(1)} %copy-done.10, bf16[128,128]{1,0:T(8,128)(2,1)S(1)} %copy-done.5), kind=kOutput, calls=%fused_computation.23 | convolution fusion | flops 75792384 | bytes 1802752 | tf_op jit(solution)/shard_map/dot_general | solution.py:74
  (36 shorter events, 0.1 us)
Async XLA Ops:
  0.0 43.2 %copy-start = (bf16[128,256]{1,0:T(8,128)(2,1)S(1)}, bf16[128,256]{1,0:T(8,128)(2,1)}, u32[]{:S(2)}) copy-start(bf16[128,256]{1,0:T(8,128)(2,1)} %param.18) | copy-start | bytes 196612
  0.0 1.8 %copy-start.1 = (f32[48,48,128]{2,1,0:T(8,128)S(1)}, f32[48,48,128]{2,1,0:T(8,128)}, u32[]{:S(2)}) copy-start(f32[48,48,128]{2,1,0:T(8,128)} %param.13) | copy-start | bytes 3538948
  0.0 2.5 %copy-start.9 = (f32[128]{0:T(128)S(1)}, f32[128]{0:T(128)}, u32[]{:S(2)}) copy-start(f32[128]{0:T(128)} %param.15) | copy-start | bytes 1540
  0.0 2.5 %copy-start.8 = (f32[128]{0:T(128)S(1)}, f32[128]{0:T(128)}, u32[]{:S(2)}) copy-start(f32[128]{0:T(128)} %param.16) | copy-start | bytes 1540
  2.5 5.8 %copy-start.7 = (f32[128,4]{0,1:T(4,128)S(1)}, f32[128,4]{0,1:T(4,128)}, u32[]{:S(2)}) copy-start(f32[128,4]{0,1:T(4,128)} %param.21) | copy-start | bytes 6148
  4.0 39.1 %all-to-all-start = ((bf16[48,48,128]{2,1,0:T(8,128)(2,1)}), bf16[48,48,128]{2,1,0:T(8,128)(2,1)S(1)}, u32[]{:S(2)}, u32[]{:S(2)}) async-start(bf16[48,48,128]{2,1,0:T(8,128)(2,1)} %add_convert_fusion), calls=%async_computation | async-start | bytes 1179648 | tf_op jit(solution)/shard_map/all_to_all | solution.py:30
  8.3 18.9 %copy-start.14 = (u32[32]{0:T(128)S(1)}, u32[32]{0:T(128)}, u32[]{:S(2)}) copy-start(u32[32]{0:T(128)} %constant.66) | copy-start | bytes 388
  8.3 20.1 %copy-start.12 = (s32[48]{0:T(128)S(1)}, s32[48]{0:T(128)}, u32[]{:S(2)}) copy-start(s32[48]{0:T(128)} %param.14) | copy-start | bytes 580
  44.3 2.1 %copy-start.6 = (bf16[128,128]{1,0:T(8,128)(2,1)S(1)}, bf16[128,128]{1,0:T(8,128)(2,1)}, u32[]{:S(2)}) copy-start(bf16[128,128]{1,0:T(8,128)(2,1)} %param.17) | copy-start | bytes 98308
  46.4 1.5 %copy-start.11 = (bf16[128,128]{1,0:T(8,128)(2,1)S(1)}, bf16[128,128]{1,0:T(8,128)(2,1)}, u32[]{:S(2)}) copy-start(bf16[128,128]{1,0:T(8,128)(2,1)} %param.19) | copy-start | bytes 98308
  46.4 1.5 %copy-start.13 = (f32[128]{0:T(128)S(1)}, f32[128]{0:T(128)}, u32[]{:S(2)}) copy-start(f32[128]{0:T(128)} %param.20) | copy-start | bytes 1540
  47.9 2.5 %copy-start.3 = (bf16[12,192,4,32]{1,3,0,2:T(8,128)(2,1)S(1)}, bf16[12,192,4,32]{1,3,0,2:T(8,128)(2,1)}, u32[]{:S(2)}) copy-start(bf16[12,192,4,32]{1,3,0,2:T(8,128)(2,1)} %copy.40) | copy-start | bytes 1769476
  55.3 2.9 %copy-start.2 = (f32[12,192,128]{2,1,0:T(8,128)S(1)}, f32[12,192,128]{2,1,0:T(8,128)}, u32[]{:S(2)}) copy-start(f32[12,192,128]{2,1,0:T(8,128)} %get-tuple-element.269) | copy-start | bytes 3538948 | tf_op jit(solution)/shard_map/while
  58.6 1.2 %copy-start.4 = (bf16[12,192,4,32]{1,3,0,2:T(8,128)(2,1)S(1)}, bf16[12,192,4,32]{1,3,0,2:T(8,128)(2,1)}, u32[]{:S(2)}) copy-start(bf16[12,192,4,32]{1,3,0,2:T(8,128)(2,1)} %get-tuple-element.292) | copy-start | bytes 1769476 | tf_op jit(solution)/shard_map/while
  64.7 2.9 %copy-start.2 = (f32[12,192,128]{2,1,0:T(8,128)S(1)}, f32[12,192,128]{2,1,0:T(8,128)}, u32[]{:S(2)}) copy-start(f32[12,192,128]{2,1,0:T(8,128)} %get-tuple-element.269) | copy-start | bytes 3538948 | tf_op jit(solution)/shard_map/while
  68.1 1.1 %copy-start.4 = (bf16[12,192,4,32]{1,3,0,2:T(8,128)(2,1)S(1)}, bf16[12,192,4,32]{1,3,0,2:T(8,128)(2,1)}, u32[]{:S(2)}) copy-start(bf16[12,192,4,32]{1,3,0,2:T(8,128)(2,1)} %get-tuple-element.292) | copy-start | bytes 1769476 | tf_op jit(solution)/shard_map/while
  69.2 15.4 %copy-start.5 = (bf16[128,128]{1,0:T(8,128)(2,1)S(1)}, bf16[128,128]{1,0:T(8,128)(2,1)}, u32[]{:S(2)}) copy-start(bf16[128,128]{1,0:T(8,128)(2,1)} %param.22) | copy-start | bytes 98308
  69.2 15.4 %copy-start.10 = (f32[128]{0:T(128)S(1)}, f32[128]{0:T(128)}, u32[]{:S(2)}) copy-start(f32[128]{0:T(128)} %param.23) | copy-start | bytes 1540
where the time goes:
time: 86.4 us; the launch traced here: 85.9 us
  blocking collectives  45.7 us (53%)
  matrix products  21 us (24%)
  local copies, waits for them, and re-layouts  9.81 us (11%)
  other arithmetic  4.24 us (5%)
  starting transfers between devices  4.24 us (5%)
    all_gather x1, blocking collectives, whole_row_layer(): bias_part = lax.all_gather(local_bias, 'cols', axis=1, tiled=True)  15.8 us
    all_to_all x1, blocking collectives, whole_row_layer(): lax.all_to_all(gated_all, 'rows', split_axis=1, concat_axis=0, tiled=True)  15.2 us
    all_gather x1, blocking collectives, whole_row_layer(): lax.all_gather(bias_part, 'rows', axis=2, tiled=True)  9.04 us
    sub x2, matrix products, one_block(): expo = jnp.exp(scores - highest)  8.86 us
    dot_general x2, matrix products, one_block(): jnp.einsum('hijk,ikhd->ijhd', weights, values, preferred_element_type=jnp...  5.81 us
    unnamed x1, blocking collectives  5.63 us
    all_to_all x1, starting transfers between devices, whole_row_layer(): lax.all_to_all(normed, 'rows', split_axis=0, concat_axis=1, tiled=True)  4.24 us
    dot_general x1, matrix products, whole_row_layer(): jnp.dot(normed.astype(jnp.float32), w_bias, precision=lax.Precision.HIGHEST)  2.85 us
  transfers between devices with their start and end apart: 1, of which 0 were waited for; matrix products, arithmetic and copies ran while one was open for 4% of the time, Pallas kernels for 0%

commit v1 on v0

v1 whole, which is shorter than its diff:
```python
import functools

import jax
import jax.numpy as jnp
from jax import lax
from jax.experimental import pallas as pl
from jax.experimental.pallas import tpu as pltpu
from jax.sharding import PartitionSpec as P

HEADS = 4
HEAD_DIM = 32
MASKED = -1000000000.0
ROWS_PER_LN_STEP = 8
ROWS_PER_STEP = 4

VMEM = pltpu.VMEM
NT = (((1,), (1,)), ((), ()))


def chunk_sizes(count):
    half = count // 2
    if count % 2 or half % ROWS_PER_LN_STEP:
        return (count,)
    return (half, count - half)


def norm_kernel(sizes, x_ref, mask_ref, gain_ref, shift_ref, w_ref, *refs):
    outs, bias_ref, w_scr = refs[:-2], refs[-2], refs[-1]
    width = x_ref.shape[1]
    lanes = ROWS_PER_LN_STEP * width
    w = w_ref[...]
    hi = w.astype(jnp.bfloat16).astype(jnp.float32)
    mid = (w - hi).astype(jnp.bfloat16).astype(jnp.float32)
    low = w - hi - mid
    w_scr[...] = jnp.zeros_like(w_scr)
    w_scr[0:HEADS, :] = hi
    w_scr[8 : 8 + HEADS, :] = mid
    w_scr[16 : 16 + HEADS, :] = low
    w3 = w_scr[...].astype(jnp.bfloat16)
    spread = (
        lax.broadcasted_iota(jnp.int32, (width, lanes), 1) % width
        == lax.broadcasted_iota(jnp.int32, (width, lanes), 0)
    ).astype(jnp.float32)
    usable = jnp.dot(
        jnp.broadcast_to(mask_ref[...].astype(jnp.float32), (8, width)).astype(jnp.bfloat16),
        spread.astype(jnp.bfloat16),
        preferred_element_type=jnp.float32,
    )
    gain, shift = gain_ref[...], shift_ref[...]
    at = 0
    for out, size in zip(outs, sizes, strict=True):
        for step in range(size // ROWS_PER_LN_STEP):
            x = x_ref[at : at + ROWS_PER_LN_STEP].reshape(lanes, x_ref.shape[2])
            centred = x - jnp.mean(x, axis=-1, keepdims=True)
            var = jnp.mean(centred * centred, axis=-1, keepdims=True)
            normed = (centred * lax.rsqrt(var + 1e-05) * gain + shift).astype(jnp.bfloat16)
            out[step * ROWS_PER_LN_STEP : (step + 1) * ROWS_PER_LN_STEP] = normed.reshape(
                ROWS_PER_LN_STEP, width, x_ref.shape[2]
            )
            parts = lax.dot_general(w3, normed, NT, preferred_element_type=jnp.float32)
            bias = parts[0:8] + parts[8:16] + parts[16:24]
            bias = jnp.where(usable > 0.5, bias, MASKED)
            bias_ref[:, at * width : at * width + lanes] = bias[0:HEADS]
            at += ROWS_PER_LN_STEP


def attend_kernel(blocks, *refs):
    x_refs = refs[:blocks]
    bias_ref, wq_ref, wkv_ref, wg_ref, gshift_ref, wout_ref, oshift_ref = refs[blocks : blocks + 7]
    out_ref = refs[-1]
    rows, width, chans = x_refs[0].shape
    keys_n = blocks * width
    own = x_refs[0][...].reshape(rows * width, chans)
    every = jnp.concatenate([x[...] for x in x_refs], axis=1).reshape(rows * keys_n, chans)
    queries = (
        jnp.dot(own, wq_ref[...], preferred_element_type=jnp.float32) * HEAD_DIM ** (-0.5)
    ).astype(jnp.bfloat16)
    gates = jax.nn.sigmoid(
        jnp.dot(own, wg_ref[...], preferred_element_type=jnp.float32) + gshift_ref[...]
    )
    keyvals = jnp.dot(every, wkv_ref[...], preferred_element_type=jnp.float32).astype(jnp.bfloat16)
    head_of_lane = lax.broadcasted_iota(jnp.int32, (width, chans), 1) // HEAD_DIM
    ones = jnp.ones((keys_n, chans), jnp.bfloat16)
    bias = bias_ref[...]
    gated = []
    for i in range(rows):
        query = queries[i * width : (i + 1) * width]
        by_head = jnp.concatenate(
            [jnp.where(head_of_lane == h, query, jnp.zeros_like(query)) for h in range(HEADS)], axis=0
        )
        key = keyvals[i * keys_n : (i + 1) * keys_n, :chans]
        value = keyvals[i * keys_n : (i + 1) * keys_n, chans:]
        scores = lax.dot_general(by_head, key, NT, preferred_element_type=jnp.float32) + bias
        expo = jnp.exp(scores - jnp.max(scores, axis=-1, keepdims=True))
        mixed = jnp.dot(
            expo.astype(jnp.bfloat16),
            jnp.concatenate([value, ones], axis=1),
            preferred_element_type=jnp.float32,
        )
        top, total = mixed[0:width, :chans], mixed[0:width, chans:]
        for h in range(1, HEADS):
            part = mixed[h * width : (h + 1) * width]
            top = jnp.where(head_of_lane == h, part[:, :chans], top)
            total = jnp.where(head_of_lane == h, part[:, chans:], total)
        gated.append((gates[i * width : (i + 1) * width] * (top / total)).astype(jnp.bfloat16))
    update = (
        jnp.dot(jnp.concatenate(gated, axis=0), wout_ref[...], preferred_element_type=jnp.float32)
        + oshift_ref[...]
    )
    out_ref[...] = update.reshape(rows, width, chans)


def whole(array):
    return pl.BlockSpec(array.shape, lambda *_: (0,) * array.ndim)


def on_device(
    n_rows,
    n_cols,
    pair_rep,
    token_mask,
    norm_gain,
    norm_shift,
    w_query,
    w_keyval,
    w_gate,
    gate_shift,
    w_bias,
    w_out,
    out_shift,
):
    own_rows, width, chans = pair_rep.shape
    sizes = chunk_sizes(own_rows)
    heads = w_bias.shape[1]
    row_vec = lambda v: v.reshape(1, -1)
    *normed, bias_own = pl.pallas_call(
        functools.partial(norm_kernel, sizes),
        out_shape=[jax.ShapeDtypeStruct((s, width, chans), jnp.bfloat16) for s in sizes]
        + [jax.ShapeDtypeStruct((heads, own_rows * width), jnp.float32)],
        scratch_shapes=[VMEM((24, chans), jnp.float32)],
        name="norm",
    )(pair_rep, row_vec(token_mask), row_vec(norm_gain), row_vec(norm_shift), w_bias.T)

    offsets = [0]
    hops = []
    step = n_rows // 2
    while step:
        hops.append(step)
        offsets += [o ^ step for o in offsets]
        step //= 2

    def gather(part):
        held = [part]
        for hop in hops:
            perm = [(r, r ^ hop) for r in range(n_rows)]
            held += [lax.ppermute(b, "rows", perm) for b in held]
        return held

    gathered = [gather(part) for part in normed]

    r_at, c_at = lax.axis_index("rows"), lax.axis_index("cols")
    if n_rows == n_cols:
        got = []
        for s in range(n_rows):
            perm = [
                (r * n_cols + c, c * n_cols + (r ^ c ^ s)) for r in range(n_rows) for c in range(n_cols)
            ]
            got.append(lax.ppermute(bias_own, ("rows", "cols"), perm))
        slots = []
        for o in offsets:
            slot = got[o]
            for c in range(1, n_cols):
                slot = jnp.where(c_at == c, got[o ^ c], slot)
            slots.append(slot.reshape(heads, width, width))
    else:
        block = lax.all_gather(bias_own.reshape(heads, own_rows, width), "cols", axis=1, tiled=True)
        block = block.reshape(heads, n_rows, width, width)
        block = lax.all_to_all(block, "rows", split_axis=1, concat_axis=1, tiled=True)
        slots = [lax.dynamic_index_in_dim(block, r_at ^ o, 1, keepdims=False) for o in offsets]
    bias = jnp.concatenate(slots, axis=2).reshape(heads * width, n_rows * width)

    small = (
        bias, w_query, w_keyval, w_gate, row_vec(gate_shift), w_out, row_vec(out_shift)
    )
    update = None
    at = 0
    for size, blocks in zip(sizes, gathered, strict=True):
        first = at // ROWS_PER_STEP
        operands = (*blocks, *small)
        in_specs = [
            pl.BlockSpec((ROWS_PER_STEP, width, chans), lambda s: (s, 0, 0)) for _ in blocks
        ] + [whole(a) for a in small]
        aliases = {}
        if update is not None:
            aliases = {len(operands): 0}
            operands += (update,)
            in_specs.append(pl.BlockSpec(memory_space=pl.ANY))
        update = pl.pallas_call(
            functools.partial(attend_kernel, len(blocks)),
            grid=(size // ROWS_PER_STEP,),
            in_specs=in_specs,
            out_specs=pl.BlockSpec((ROWS_PER_STEP, width, chans), lambda s, first=first: (first + s, 0, 0)),
            out_shape=jax.ShapeDtypeStruct(pair_rep.shape, jnp.float32),
            input_output_aliases=aliases,
            name="attend",
        )(*operands)
        at += size
    return update


def solution(mesh):
    return jax.shard_map(
        functools.partial(on_device, mesh.shape["rows"], mesh.shape["cols"]),
        mesh=mesh,
        in_specs=(
            P(("groups", "cols"), "rows", None),
            P(("groups", "rows")),
            P(),
            P(),
            P(),
            P(),
            P(),
            P(),
            P(),
            P(),
            P(),
        ),
        out_specs=P(("groups", "cols"), "rows", None),
        check_vma=False,
    )
```

time: 86.4 us -> 48.4 us (0.56)
  blocking collectives: 45.7 us -> 0 us
  matrix products: 21 us -> 0 us
  starting transfers between devices: 4.24 us -> 24 us
  Pallas kernels: 0 us -> 19.5 us
  local copies, waits for them, and re-layouts: 9.81 us -> 2.65 us
  other arithmetic: 4.24 us -> 0.92 us
    all_gather x2 -> x0, blocking collectives: 24.9 us -> none  [the longest x1 15.8 us: whole_row_layer(): bias_part = lax.all_gather(local_bias, 'cols', axis=1, tiled=True)]
    ppermute x0 -> x10, starting transfers between devices: none -> 24 us  [the longest x4 19.9 us: on_device(): got.append(lax.ppermute(bias_own, ('rows', 'cols'), perm))]
    pallas_call x0 -> x3, Pallas kernels: none -> 19.5 us  [the longest x2 16.6 us: on_device(): pl.pallas_call(functools.partial(attend_kernel, len(blocks)), grid=(size...]
    all_to_all x1 -> x0, blocking collectives: 15.2 us -> none  [whole_row_layer(): lax.all_to_all(gated_all, 'rows', split_axis=1, concat_axis=0, tiled=True)]
    dot_general x7 -> x0, matrix products: 12.2 us -> none  [the longest x2 5.81 us: one_block(): jnp.einsum('hijk,ikhd->ijhd', weights, values, preferred_element_type=jnp...]
    sub x2 -> x0, matrix products: 8.86 us -> none  [one_block(): expo = jnp.exp(scores - highest)]
    unnamed x1 -> x0, blocking collectives: 5.63 us -> none
    all_to_all x1 -> x0, starting transfers between devices: 4.24 us -> none  [whole_row_layer(): lax.all_to_all(normed, 'rows', split_axis=0, concat_axis=1, tiled=True)]
  transfers between devices with their start and end apart: 1 -> 10, of which waited for: 0 -> 1; matrix products, arithmetic and copies ran while one was open for 4% -> 3% of each run, Pallas kernels for 0% -> 17%
where the time goes in v1:
time: 48.4 us; the launch traced here: 48 us
  starting transfers between devices  24 us (50%)
  Pallas kernels  19.5 us (40%)
  local copies, waits for them, and re-layouts  2.65 us (5%)
  other arithmetic  0.92 us (2%)
  waiting for transfers between devices  0.83 us (2%)
    ppermute x4, starting transfers between devices, on_device(): got.append(lax.ppermute(bias_own, ('rows', 'cols'), perm))  19.9 us
    pallas_call x2, Pallas kernels, on_device(): pl.pallas_call(functools.partial(attend_kernel, len(blocks)), grid=(size...  16.6 us
    ppermute x6, starting transfers between devices, gather(): held += [lax.ppermute(b, 'rows', perm) for b in held]  4.06 us
    pallas_call x1, Pallas kernels, on_device(): pl.pallas_call(functools.partial(norm_kernel, sizes), out_shape=[jax.Shap...  2.85 us
    unnamed x12, local copies, waits for them, and re-layouts  2.23 us
  transfers between devices with their start and end apart: 10, of which 1 were waited for; matrix products, arithmetic and copies ran while one was open for 3% of the time, Pallas kernels for 17%

profile of v1, /device:TPU:0, one launch (start us, length us, event | category | flops | bytes accessed | tf_op | source)
XLA Modules:
  0.0 48.0 jit_solution(7862684260434610773)
XLA Ops:
  0.0 2.9 %norm.1 = (bf16[24,48,128]{2,1,0:T(8,128)(2,1)}, bf16[24,48,128]{2,1,0:T(8,128)(2,1)}, f32[4,2304]{1,0:T(4,128)}) custom-call(f32[48,48,128]{2,1,0:T(8,128)} %x_ref.1, s32[1,48]{1,0:T(1,128)} %bitcast.11, f32[1,128]{1,0:T(1,128)} %bitcast.12, f32[1,128]{1,0:T(1,128)} %bitcast.13, f32[4,128]{1,0:T(4,128)} %bitcast.6), custom_call_target="tpu_custom_call" | custom-call | tf_op jit(solution)/shard_map/norm/pallas_call | solution.py:136
  2.9 3.0 %collective-permute-start = (bf16[24,48,128]{2,1,0:T(8,128)(2,1)}, bf16[24,48,128]{2,1,0:T(8,128)(2,1)S(1)}, u32[]{:S(2)}, u32[]{:S(2)}) collective-permute-start(bf16[24,48,128]{2,1,0:T(8,128)(2,1)} %get-tuple-element.8.refs_0_), channel_id=1, source_target_pairs={{0,8},{4,12},{8,0},{12,4},{1,9},{5,13},{9,1},{13,5},{2,10},{6,14},... | collective-permute-start | bytes 884744 | tf_op jit(solution)/shard_map/ppermute | solution.py:156
  5.8 0.0 collective-permute-start.7
  5.8 1.4 %collective-permute-start.6 = (f32[4,2304]{1,0:T(4,128)}, f32[4,2304]{1,0:T(4,128)S(1)}, u32[]{:S(2)}, u32[]{:S(2)}) collective-permute-start(f32[4,2304]{1,0:T(4,128)} %get-tuple-element.9), channel_id=1, source_target_pairs={{0,0},{1,5},{2,10},{3,15},{4,1},{5,4},{6,11},{7,14},{8,2},{9,7},{1... | collective-permute-start | bytes 110600 | tf_op jit(solution)/shard_map/ppermute | solution.py:168
  7.3 4.5 %collective-permute-start.5 = (f32[4,2304]{1,0:T(4,128)}, f32[4,2304]{1,0:T(4,128)S(1)}, u32[]{:S(2)}, u32[]{:S(2)}) collective-permute-start(f32[4,2304]{1,0:T(4,128)} %get-tuple-element.9), channel_id=1, source_target_pairs={{0,1},{1,4},{2,11},{3,14},{4,0},{5,5},{6,10},{7,15},{8,3},{9,6},{1... | collective-permute-start | bytes 110600 | tf_op jit(solution)/shard_map/ppermute | solution.py:168
  11.8 5.4 %collective-permute-start.4 = (f32[4,2304]{1,0:T(4,128)}, f32[4,2304]{1,0:T(4,128)S(1)}, u32[]{:S(2)}, u32[]{:S(2)}) collective-permute-start(f32[4,2304]{1,0:T(4,128)} %get-tuple-element.9), channel_id=1, source_target_pairs={{0,2},{1,7},{2,8},{3,13},{4,3},{5,6},{6,9},{7,12},{8,0},{9,5},{10,... | collective-permute-start | bytes 110600 | tf_op jit(solution)/shard_map/ppermute | solution.py:168
  17.2 0.0 collective-permute-done.6
  17.2 8.6 %collective-permute-start.3 = (f32[4,2304]{1,0:T(4,128)}, f32[4,2304]{1,0:T(4,128)S(1)}, u32[]{:S(2)}, u32[]{:S(2)}) collective-permute-start(f32[4,2304]{1,0:T(4,128)} %get-tuple-element.9), channel_id=1, source_target_pairs={{0,3},{1,6},{2,9},{3,12},{4,2},{5,7},{6,8},{7,13},{8,1},{9,4},{10,... | collective-permute-start | bytes 110600 | tf_op jit(solution)/shard_map/ppermute | solution.py:168
  25.8 0.0 collective-permute-done.5
  25.8 0.1 collective-permute-start.1
  25.9 0.0 collective-permute-done.4
  25.9 0.5 %collective-permute-start.8 = (bf16[24,48,128]{2,1,0:T(8,128)(2,1)}, bf16[24,48,128]{2,1,0:T(8,128)(2,1)S(1)}, u32[]{:S(2)}, u32[]{:S(2)}) collective-permute-start(bf16[24,48,128]{2,1,0:T(8,128)(2,1)} %get-tuple-element.10.refs_0_), channel_id=1, source_target_pairs={{0,4},{4,0},{8,12},{12,8},{1,5},{5,1},{9,13},{13,9},{2,6},{6,2},{1... | collective-permute-start | bytes 884744 | tf_op jit(solution)/shard_map/ppermute | solution.py:156
  26.4 0.0 collective-permute-done.refs_1_
  26.4 0.0 copy-start
  26.4 0.1 collective-permute-start.2
  26.5 0.0 collective-permute-done.7.refs_1_
  26.5 0.0 copy-start.1
  26.5 0.4 collective-permute-start.9
  26.9 0.8 %collective-permute-done.3 = f32[4,2304]{1,0:T(4,128)S(1)} collective-permute-done((f32[4,2304]{1,0:T(4,128)}, f32[4,2304]{1,0:T(4,128)S(1)}, u32[]{:S(2)}, u32[]{:S(2)}) %collective-permute-start.3) | collective-permute-done | bytes 36896 | tf_op jit(solution)/shard_map/ppermute | solution.py:168
  27.8 0.1 concatenate.12
  27.9 0.1 concatenate.15
  28.0 0.1 concatenate.14
  28.1 0.1 concatenate.13
  28.2 0.9 %pad_maximum_fusion.refs_4_ = f32[192,192]{1,0:T(8,128)} fusion(f32[192,48]{1,0:T(8,128)S(1)} %concatenate.15, f32[192,48]{1,0:T(8,128)S(1)} %concatenate.14, f32[192,48]{1,0:T(8,128)S(1)} %concatenate.13, f32[192,48]{1,0:T(8,128)S(1)} %concatenate.12), kind=kLoop, calls=%fused_computation | loop fusion | flops 110592 | bytes 294912 | tf_op jit(solution)/shard_map/concatenate | solution.py:180
  29.1 0.0 collective-permute-done.8.refs_2_
  29.1 0.0 copy-start.4
  29.1 0.0 collective-permute-done.9.refs_3_
  29.1 0.0 copy-start.5
  29.1 0.0 copy-done.1
  29.1 0.7 %copy-done.4 = bf16[24,48,128]{2,1,0:T(8,128)(2,1)} copy-done((bf16[24,48,128]{2,1,0:T(8,128)(2,1)}, bf16[24,48,128]{2,1,0:T(8,128)(2,1)S(1)}, u32[]{:S(2)}) %copy-start.4) | copy-done | bytes 294936
  29.8 0.1 copy-done.5
  30.0 8.3 %attend.2.refs_11_ = f32[48,48,128]{2,1,0:T(8,128)} custom-call(bf16[24,48,128]{2,1,0:T(8,128)(2,1)} %get-tuple-element.10.refs_0_, bf16[24,48,128]{2,1,0:T(8,128)(2,1)} %copy-done.1, bf16[24,48,128]{2,1,0:T(8,128)(2,1)} %copy-done.4, bf16[24,48,128]{2,1,0:T(8,128)(2,1)} %copy-done.5, f32[192,192]{1,0:T(8,128)} %pad_maximum_fusion.refs_4_, ...), custom_call_target="tpu_custom_call" | custom-call | tf_op jit(solution)/shard_map/attend/pallas_call | solution.py:198
  38.3 0.0 copy-done
  38.3 0.0 collective-permute-done.1.refs_2_
  38.3 0.0 copy-start.2
  38.3 0.0 collective-permute-done.2.refs_3_
  38.3 0.7 %copy-done.2 = bf16[24,48,128]{2,1,0:T(8,128)(2,1)} copy-done((bf16[24,48,128]{2,1,0:T(8,128)(2,1)}, bf16[24,48,128]{2,1,0:T(8,128)(2,1)S(1)}, u32[]{:S(2)}) %copy-start.2) | copy-done | bytes 294936
  39.0 0.0 copy-start.3
  39.0 0.7 %copy-done.3 = bf16[24,48,128]{2,1,0:T(8,128)(2,1)} copy-done((bf16[24,48,128]{2,1,0:T(8,128)(2,1)}, bf16[24,48,128]{2,1,0:T(8,128)(2,1)S(1)}, u32[]{:S(2)}) %copy-start.3) | copy-done | bytes 294936
  39.7 8.3 %attend.3 = f32[48,48,128]{2,1,0:T(8,128)} custom-call(bf16[24,48,128]{2,1,0:T(8,128)(2,1)} %get-tuple-element.8.refs_0_, bf16[24,48,128]{2,1,0:T(8,128)(2,1)} %copy-done, bf16[24,48,128]{2,1,0:T(8,128)(2,1)} %copy-done.2, bf16[24,48,128]{2,1,0:T(8,128)(2,1)} %copy-done.3, f32[192,192]{1,0:T(8,128)} %pad_maximum_fusion.refs_4_, ...), custom_call_target="tpu_custom_call", output_to_operand_aliasing={{}: (11, {})} | custom-call | tf_op jit(solution)/shard_map/attend/pallas_call | solution.py:198
  (1 shorter events, 0.0 us)
Async XLA Ops:
  2.9 23.6 %collective-permute-start = (bf16[24,48,128]{2,1,0:T(8,128)(2,1)}, bf16[24,48,128]{2,1,0:T(8,128)(2,1)S(1)}, u32[]{:S(2)}, u32[]{:S(2)}) collective-permute-start(bf16[24,48,128]{2,1,0:T(8,128)(2,1)} %get-tuple-element.8.refs_0_), channel_id=1, source_target_pairs={{0,8},{4,12},{8,0},{12,4},{1,9},{5,13},{9,1},{13,5},{2,10},{6,14},... | collective-permute-start | bytes 884744 | tf_op jit(solution)/shard_map/ppermute | solution.py:156
  5.8 20.7 %collective-permute-start.7 = (bf16[24,48,128]{2,1,0:T(8,128)(2,1)}, bf16[24,48,128]{2,1,0:T(8,128)(2,1)S(1)}, u32[]{:S(2)}, u32[]{:S(2)}) collective-permute-start(bf16[24,48,128]{2,1,0:T(8,128)(2,1)} %get-tuple-element.10.refs_0_), channel_id=1, source_target_pairs={{0,8},{4,12},{8,0},{12,4},{1,9},{5,13},{9,1},{13,5},{2,10},{6,14},... | collective-permute-start | bytes 884744 | tf_op jit(solution)/shard_map/ppermute | solution.py:156
  5.8 11.4 %collective-permute-start.6 = (f32[4,2304]{1,0:T(4,128)}, f32[4,2304]{1,0:T(4,128)S(1)}, u32[]{:S(2)}, u32[]{:S(2)}) collective-permute-start(f32[4,2304]{1,0:T(4,128)} %get-tuple-element.9), channel_id=1, source_target_pairs={{0,0},{1,5},{2,10},{3,15},{4,1},{5,4},{6,11},{7,14},{8,2},{9,7},{1... | collective-permute-start | bytes 110600 | tf_op jit(solution)/shard_map/ppermute | solution.py:168
  7.3 18.6 %collective-permute-start.5 = (f32[4,2304]{1,0:T(4,128)}, f32[4,2304]{1,0:T(4,128)S(1)}, u32[]{:S(2)}, u32[]{:S(2)}) collective-permute-start(f32[4,2304]{1,0:T(4,128)} %get-tuple-element.9), channel_id=1, source_target_pairs={{0,1},{1,4},{2,11},{3,14},{4,0},{5,5},{6,10},{7,15},{8,3},{9,6},{1... | collective-permute-start | bytes 110600 | tf_op jit(solution)/shard_map/ppermute | solution.py:168
  11.8 14.1 %collective-permute-start.4 = (f32[4,2304]{1,0:T(4,128)}, f32[4,2304]{1,0:T(4,128)S(1)}, u32[]{:S(2)}, u32[]{:S(2)}) collective-permute-start(f32[4,2304]{1,0:T(4,128)} %get-tuple-element.9), channel_id=1, source_target_pairs={{0,2},{1,7},{2,8},{3,13},{4,3},{5,6},{6,9},{7,12},{8,0},{9,5},{10,... | collective-permute-start | bytes 110600 | tf_op jit(solution)/shard_map/ppermute | solution.py:168
  17.2 10.5 %collective-permute-start.3 = (f32[4,2304]{1,0:T(4,128)}, f32[4,2304]{1,0:T(4,128)S(1)}, u32[]{:S(2)}, u32[]{:S(2)}) collective-permute-start(f32[4,2304]{1,0:T(4,128)} %get-tuple-element.9), channel_id=1, source_target_pairs={{0,3},{1,6},{2,9},{3,12},{4,2},{5,7},{6,8},{7,13},{8,1},{9,4},{10,... | collective-permute-start | bytes 110600 | tf_op jit(solution)/shard_map/ppermute | solution.py:168
  25.8 12.5 %collective-permute-start.1 = (bf16[24,48,128]{2,1,0:T(8,128)(2,1)}, bf16[24,48,128]{2,1,0:T(8,128)(2,1)S(1)}, u32[]{:S(2)}, u32[]{:S(2)}) collective-permute-start(bf16[24,48,128]{2,1,0:T(8,128)(2,1)} %get-tuple-element.8.refs_0_), channel_id=1, source_target_pairs={{0,4},{4,0},{8,12},{12,8},{1,5},{5,1},{9,13},{13,9},{2,6},{6,2},{1... | collective-permute-start | bytes 884744 | tf_op jit(solution)/shard_map/ppermute | solution.py:156
  25.9 3.2 %collective-permute-start.8 = (bf16[24,48,128]{2,1,0:T(8,128)(2,1)}, bf16[24,48,128]{2,1,0:T(8,128)(2,1)S(1)}, u32[]{:S(2)}, u32[]{:S(2)}) collective-permute-start(bf16[24,48,128]{2,1,0:T(8,128)(2,1)} %get-tuple-element.10.refs_0_), channel_id=1, source_target_pairs={{0,4},{4,0},{8,12},{12,8},{1,5},{5,1},{9,13},{13,9},{2,6},{6,2},{1... | collective-permute-start | bytes 884744 | tf_op jit(solution)/shard_map/ppermute | solution.py:156
  26.4 11.9 %copy-start = (bf16[24,48,128]{2,1,0:T(8,128)(2,1)}, bf16[24,48,128]{2,1,0:T(8,128)(2,1)S(1)}, u32[]{:S(2)}) copy-start(bf16[24,48,128]{2,1,0:T(8,128)(2,1)S(1)} %collective-permute-done.refs_1_) | copy-start | bytes 884740
  26.4 11.9 %collective-permute-start.2 = (bf16[24,48,128]{2,1,0:T(8,128)(2,1)S(1)}, bf16[24,48,128]{2,1,0:T(8,128)(2,1)S(1)}, u32[]{:S(2)}, u32[]{:S(2)}) collective-permute-start(bf16[24,48,128]{2,1,0:T(8,128)(2,1)S(1)} %collective-permute-done.refs_1_), channel_id=1, source_target_pairs={{0,4},{4,0},{8,12},{12,8},{1,5},{5,1},{9,13},{13,9},{2,6},{6,2},{1... | collective-permute-start | bytes 884744 | tf_op jit(solution)/shard_map/ppermute | solution.py:156
  26.5 2.6 %copy-start.1 = (bf16[24,48,128]{2,1,0:T(8,128)(2,1)}, bf16[24,48,128]{2,1,0:T(8,128)(2,1)S(1)}, u32[]{:S(2)}) copy-start(bf16[24,48,128]{2,1,0:T(8,128)(2,1)S(1)} %collective-permute-done.7.refs_1_) | copy-start | bytes 884740
  26.5 2.6 %collective-permute-start.9 = (bf16[24,48,128]{2,1,0:T(8,128)(2,1)S(1)}, bf16[24,48,128]{2,1,0:T(8,128)(2,1)S(1)}, u32[]{:S(2)}, u32[]{:S(2)}) collective-permute-start(bf16[24,48,128]{2,1,0:T(8,128)(2,1)S(1)} %collective-permute-done.7.refs_1_), channel_id=1, source_target_pairs={{0,4},{4,0},{8,12},{12,8},{1,5},{5,1},{9,13},{13,9},{2,6},{6,2},{1... | collective-permute-start | bytes 884744 | tf_op jit(solution)/shard_map/ppermute | solution.py:156
  29.1 0.7 %copy-start.4 = (bf16[24,48,128]{2,1,0:T(8,128)(2,1)}, bf16[24,48,128]{2,1,0:T(8,128)(2,1)S(1)}, u32[]{:S(2)}) copy-start(bf16[24,48,128]{2,1,0:T(8,128)(2,1)S(1)} %collective-permute-done.8.refs_2_) | copy-start | bytes 884740
  29.1 0.8 %copy-start.5 = (bf16[24,48,128]{2,1,0:T(8,128)(2,1)}, bf16[24,48,128]{2,1,0:T(8,128)(2,1)S(1)}, u32[]{:S(2)}) copy-start(bf16[24,48,128]{2,1,0:T(8,128)(2,1)S(1)} %collective-permute-done.9.refs_3_) | copy-start | bytes 884740
  38.3 0.7 %copy-start.2 = (bf16[24,48,128]{2,1,0:T(8,128)(2,1)}, bf16[24,48,128]{2,1,0:T(8,128)(2,1)S(1)}, u32[]{:S(2)}) copy-start(bf16[24,48,128]{2,1,0:T(8,128)(2,1)S(1)} %collective-permute-done.1.refs_2_) | copy-start | bytes 884740
  39.0 0.7 %copy-start.3 = (bf16[24,48,128]{2,1,0:T(8,128)(2,1)}, bf16[24,48,128]{2,1,0:T(8,128)(2,1)S(1)}, u32[]{:S(2)}) copy-start(bf16[24,48,128]{2,1,0:T(8,128)(2,1)S(1)} %collective-permute-done.2.refs_3_) | copy-start | bytes 884740

commit v2 on v1

--- a/solution.py
+++ b/solution.py
@@ -11,10 +11,13 @@
 HEAD_DIM = 32
 MASKED = -1000000000.0
 ROWS_PER_LN_STEP = 8
-ROWS_PER_STEP = 4
 
 VMEM = pltpu.VMEM
 NT = (((1,), (1,)), ((), ()))
+
+
+def largest_divisor(count, limit):
+    return max(d for d in range(1, min(count, limit) + 1) if count % d == 0)
 
 
 def chunk_sizes(count):
@@ -64,50 +67,73 @@
             at += ROWS_PER_LN_STEP
 
 
-def attend_kernel(blocks, *refs):
+def attend_kernel(blocks, group, first, *refs):
     x_refs = refs[:blocks]
     bias_ref, wq_ref, wkv_ref, wg_ref, gshift_ref, wout_ref, oshift_ref = refs[blocks : blocks + 7]
-    out_ref = refs[-1]
+    out_ref, k_scr, v_scr, q_scr, g_scr, a_scr, o_scr, sem = refs[-8:]
     rows, width, chans = x_refs[0].shape
     keys_n = blocks * width
-    own = x_refs[0][...].reshape(rows * width, chans)
-    every = jnp.concatenate([x[...] for x in x_refs], axis=1).reshape(rows * keys_n, chans)
-    queries = (
-        jnp.dot(own, wq_ref[...], preferred_element_type=jnp.float32) * HEAD_DIM ** (-0.5)
-    ).astype(jnp.bfloat16)
-    gates = jax.nn.sigmoid(
-        jnp.dot(own, wg_ref[...], preferred_element_type=jnp.float32) + gshift_ref[...]
-    )
-    keyvals = jnp.dot(every, wkv_ref[...], preferred_element_type=jnp.float32).astype(jnp.bfloat16)
     head_of_lane = lax.broadcasted_iota(jnp.int32, (width, chans), 1) // HEAD_DIM
+    head_of_query = lax.broadcasted_iota(jnp.int32, (group, width, chans), 2) // HEAD_DIM
     ones = jnp.ones((keys_n, chans), jnp.bfloat16)
-    bias = bias_ref[...]
-    gated = []
-    for i in range(rows):
-        query = queries[i * width : (i + 1) * width]
-        by_head = jnp.concatenate(
-            [jnp.where(head_of_lane == h, query, jnp.zeros_like(query)) for h in range(HEADS)], axis=0
+
+    def do_group(start):
+        at = pl.ds(start, group)
+        own = x_refs[0][at].reshape(group * width, chans)
+        queries = (
+            (jnp.dot(own, wq_ref[...], preferred_element_type=jnp.float32) * HEAD_DIM ** (-0.5))
+            .astype(jnp.bfloat16)
+            .reshape(group, width, chans)
         )
-        key = keyvals[i * keys_n : (i + 1) * keys_n, :chans]
-        value = keyvals[i * keys_n : (i + 1) * keys_n, chans:]
-        scores = lax.dot_general(by_head, key, NT, preferred_element_type=jnp.float32) + bias
-        expo = jnp.exp(scores - jnp.max(scores, axis=-1, keepdims=True))
-        mixed = jnp.dot(
-            expo.astype(jnp.bfloat16),
-            jnp.concatenate([value, ones], axis=1),
-            preferred_element_type=jnp.float32,
+        for h in range(HEADS):
+            q_scr[at, h * width : (h + 1) * width] = jnp.where(
+                head_of_query == h, queries, jnp.zeros_like(queries)
+            )
+        gates = jnp.dot(own, wg_ref[...], preferred_element_type=jnp.float32) + gshift_ref[...]
+        g_scr[at] = jax.nn.sigmoid(gates).reshape(group, width, chans)
+        for t, x in enumerate(x_refs):
+            keyvals = (
+                jnp.dot(
+                    x[at].reshape(group * width, chans), wkv_ref[...], preferred_element_type=jnp.float32
+                )
+                .astype(jnp.bfloat16)
+                .reshape(group, width, 2 * chans)
+            )
+            k_scr[at, t * width : (t + 1) * width] = keyvals[:, :, :chans]
+            v_scr[at, t * width : (t + 1) * width] = keyvals[:, :, chans:]
+        for u in range(group):
+            i = start + u
+            scores = (
+                lax.dot_general(q_scr[i], k_scr[i], NT, preferred_element_type=jnp.float32)
+                + bias_ref[...]
+            )
+            expo = jnp.exp(scores - jnp.max(scores, axis=-1, keepdims=True))
+            mixed = jnp.dot(
+                expo.astype(jnp.bfloat16),
+                jnp.concatenate([v_scr[i], ones], axis=1),
+                preferred_element_type=jnp.float32,
+            )
+            top, total = mixed[0:width, :chans], mixed[0:width, chans:]
+            for h in range(1, HEADS):
+                part = mixed[h * width : (h + 1) * width]
+                top = jnp.where(head_of_lane == h, part[:, :chans], top)
+                total = jnp.where(head_of_lane == h, part[:, chans:], total)
+            a_scr[i] = (g_scr[i] * (top / total)).astype(jnp.bfloat16)
+        update = (
+            jnp.dot(
+                a_scr[at].reshape(group * width, chans), wout_ref[...], preferred_element_type=jnp.float32
+            )
+            + oshift_ref[...]
         )
-        top, total = mixed[0:width, :chans], mixed[0:width, chans:]
-        for h in range(1, HEADS):
-            part = mixed[h * width : (h + 1) * width]
-            top = jnp.where(head_of_lane == h, part[:, :chans], top)
-            total = jnp.where(head_of_lane == h, part[:, chans:], total)
-        gated.append((gates[i * width : (i + 1) * width] * (top / total)).astype(jnp.bfloat16))
-    update = (
-        jnp.dot(jnp.concatenate(gated, axis=0), wout_ref[...], preferred_element_type=jnp.float32)
-        + oshift_ref[...]
-    )
-    out_ref[...] = update.reshape(rows, width, chans)
+        o_scr[at] = update.reshape(group, width, chans)
+
+    if rows == group:
+        do_group(0)
+    else:
+        lax.fori_loop(0, rows // group, lambda step, _: do_group(step * group) or 0, 0)
+    copy = pltpu.make_async_copy(o_scr, out_ref.at[pl.ds(first, rows)], sem)
+    copy.start()
+    copy.wait()
 
 
 def whole(array):
@@ -159,18 +185,19 @@
     gathered = [gather(part) for part in normed]
 
     r_at, c_at = lax.axis_index("rows"), lax.axis_index("cols")
-    if n_rows == n_cols:
-        got = []
-        for s in range(n_rows):
-            perm = [
-                (r * n_cols + c, c * n_cols + (r ^ c ^ s)) for r in range(n_rows) for c in range(n_cols)
-            ]
-            got.append(lax.ppermute(bias_own, ("rows", "cols"), perm))
+    if n_rows == n_cols and n_rows & (n_rows - 1) == 0:
+        held = [bias_own]
+        for hop in [1 << k for k in range(n_cols.bit_length() - 1)]:
+            perm = [(c, c ^ hop) for c in range(n_cols)]
+            held += [lax.ppermute(b, "cols", perm) for b in held]
+        at_both = r_at ^ c_at
         slots = []
         for o in offsets:
-            slot = got[o]
-            for c in range(1, n_cols):
-                slot = jnp.where(c_at == c, got[o ^ c], slot)
+            slot = held[o]
+            for v in range(1, n_cols):
+                slot = jnp.where(at_both == v, held[o ^ v], slot)
+            if o:
+                slot = lax.ppermute(slot, "rows", [(r, r ^ o) for r in range(n_rows)])
             slots.append(slot.reshape(heads, width, width))
     else:
         block = lax.all_gather(bias_own.reshape(heads, own_rows, width), "cols", axis=1, tiled=True)
@@ -179,28 +206,34 @@
         slots = [lax.dynamic_index_in_dim(block, r_at ^ o, 1, keepdims=False) for o in offsets]
     bias = jnp.concatenate(slots, axis=2).reshape(heads * width, n_rows * width)
 
-    small = (
-        bias, w_query, w_keyval, w_gate, row_vec(gate_shift), w_out, row_vec(out_shift)
-    )
+    small = (bias, w_query, w_keyval, w_gate, row_vec(gate_shift), w_out, row_vec(out_shift))
+    in_vmem, in_place = pl.BlockSpec(memory_space=pltpu.VMEM), pl.BlockSpec(memory_space=pl.ANY)
     update = None
     at = 0
     for size, blocks in zip(sizes, gathered, strict=True):
-        first = at // ROWS_PER_STEP
         operands = (*blocks, *small)
-        in_specs = [
-            pl.BlockSpec((ROWS_PER_STEP, width, chans), lambda s: (s, 0, 0)) for _ in blocks
-        ] + [whole(a) for a in small]
+        in_specs = [in_vmem] * len(operands)
         aliases = {}
         if update is not None:
             aliases = {len(operands): 0}
             operands += (update,)
-            in_specs.append(pl.BlockSpec(memory_space=pl.ANY))
+            in_specs.append(in_place)
+        keys_n = width * len(blocks)
+        group = largest_divisor(size, max(1, 96 // len(blocks)))
         update = pl.pallas_call(
-            functools.partial(attend_kernel, len(blocks)),
-            grid=(size // ROWS_PER_STEP,),
+            functools.partial(attend_kernel, len(blocks), group, at),
             in_specs=in_specs,
-            out_specs=pl.BlockSpec((ROWS_PER_STEP, width, chans), lambda s, first=first: (first + s, 0, 0)),
+            out_specs=in_place,
             out_shape=jax.ShapeDtypeStruct(pair_rep.shape, jnp.float32),
+            scratch_shapes=[
+                VMEM((size, keys_n, chans), jnp.bfloat16),
+                VMEM((size, keys_n, chans), jnp.bfloat16),
+                VMEM((size, heads * width, chans), jnp.bfloat16),
+                VMEM((size, width, chans), jnp.float32),
+                VMEM((size, width, chans), jnp.bfloat16),
+                VMEM((size, width, chans), jnp.float32),
+                pltpu.SemaphoreType.DMA,
+            ],
             input_output_aliases=aliases,
             name="attend",
         )(*operands)

time: 48.4 us -> 41.9 us (0.87)
  waiting for transfers between devices: 0.83 us -> 11.4 us
  starting transfers between devices: 24 us -> 13.6 us
  Pallas kernels: 19.5 us -> 12.2 us
  other arithmetic: 0.92 us -> 1.74 us
    ppermute x4 -> x6, starting transfers between devices: 19.9 us -> 10.1 us  [the longest x3 7.26 us: on_device(): held += [lax.ppermute(b, 'cols', perm) for b in held]]
    pallas_call x2, Pallas kernels: 16.6 us -> 9.31 us  [on_device(): pl.pallas_call(functools.partial(attend_kernel, len(blocks), group, at),...]
    ppermute x4 -> x6, waiting for transfers between devices: 0.82 us -> 6.68 us  [the longest x3 5.68 us: on_device(): slot = lax.ppermute(slot, 'rows', [(r, r ^ o) for r in range(n_rows)])]
    ppermute x6, waiting for transfers between devices: 0.02 us -> 4.73 us  [gather(): held += [lax.ppermute(b, 'rows', perm) for b in held]]
    select_n x1, other arithmetic: 0.04 us -> 0.85 us  [on_device(): slot = jnp.where(at_both == v, held[o ^ v], slot)]
    ppermute x6, starting transfers between devices: 4.06 us -> 3.5 us  [gather(): held += [lax.ppermute(b, 'rows', perm) for b in held]]
  transfers between devices with their start and end apart: 10 -> 12, of which waited for: 1 -> 5; matrix products, arithmetic and copies ran while one was open for 3% -> 5% of each run, Pallas kernels for 17% -> 11%
where the time goes in v2:
time: 41.9 us; the launch traced here: 41.7 us
  starting transfers between devices  13.6 us (32%)
  Pallas kernels  12.2 us (29%)
  waiting for transfers between devices  11.4 us (27%)
  local copies, waits for them, and re-layouts  2.65 us (6%)
  other arithmetic  1.74 us (4%)
    pallas_call x2, Pallas kernels, on_device(): pl.pallas_call(functools.partial(attend_kernel, len(blocks), group, at),...  9.31 us
    ppermute x3, starting transfers between devices, on_device(): held += [lax.ppermute(b, 'cols', perm) for b in held]  7.26 us
    ppermute x3, waiting for transfers between devices, on_device(): slot = lax.ppermute(slot, 'rows', [(r, r ^ o) for r in range(n_rows)])  5.68 us
    ppermute x6, waiting for transfers between devices, gather(): held += [lax.ppermute(b, 'rows', perm) for b in held]  4.73 us
    ppermute x6, starting transfers between devices, gather(): held += [lax.ppermute(b, 'rows', perm) for b in held]  3.5 us
    pallas_call x1, Pallas kernels, on_device(): pl.pallas_call(functools.partial(norm_kernel, sizes), out_shape=[jax.Shap...  2.85 us
    ppermute x3, starting transfers between devices, on_device(): slot = lax.ppermute(slot, 'rows', [(r, r ^ o) for r in range(n_rows)])  2.81 us
    unnamed x12, local copies, waits for them, and re-layouts  2.23 us
  transfers between devices with their start and end apart: 12, of which 5 were waited for; matrix products, arithmetic and copies ran while one was open for 5% of the time, Pallas kernels for 11%

profile of v2, /device:TPU:0, one launch (start us, length us, event | category | flops | bytes accessed | tf_op | source)
XLA Modules:
  0.0 41.7 jit_solution(11553163615303293612)
XLA Ops:
  0.0 2.9 %norm.1 = (bf16[24,48,128]{2,1,0:T(8,128)(2,1)}, bf16[24,48,128]{2,1,0:T(8,128)(2,1)}, f32[4,2304]{1,0:T(4,128)}) custom-call(f32[48,48,128]{2,1,0:T(8,128)} %x_ref.1, s32[1,48]{1,0:T(1,128)} %bitcast.11, f32[1,128]{1,0:T(1,128)} %bitcast.12, f32[1,128]{1,0:T(1,128)} %bitcast.13, f32[4,128]{1,0:T(4,128)} %bitcast.6), custom_call_target="tpu_custom_call" | custom-call | tf_op jit(solution)/shard_map/norm/pallas_call | solution.py:162
  2.9 3.0 %collective-permute-start = (bf16[24,48,128]{2,1,0:T(8,128)(2,1)}, bf16[24,48,128]{2,1,0:T(8,128)(2,1)S(1)}, u32[]{:S(2)}, u32[]{:S(2)}) collective-permute-start(bf16[24,48,128]{2,1,0:T(8,128)(2,1)} %get-tuple-element.8.refs_0_), channel_id=1, source_target_pairs={{0,8},{4,12},{8,0},{12,4},{1,9},{5,13},{9,1},{13,5},{2,10},{6,14},... | collective-permute-start | bytes 884744 | tf_op jit(solution)/shard_map/ppermute | solution.py:182
  5.8 0.0 collective-permute-start.9
  5.8 2.1 %collective-permute-start.3 = (f32[4,2304]{1,0:T(4,128)}, f32[4,2304]{1,0:T(4,128)S(1)}, u32[]{:S(2)}, u32[]{:S(2)}) collective-permute-start(f32[4,2304]{1,0:T(4,128)} %get-tuple-element.9), channel_id=1, source_target_pairs={{0,1},{1,0},{2,3},{3,2},{4,5},{5,4},{6,7},{7,6},{8,9},{9,8},{10,11... | collective-permute-start | bytes 110600 | tf_op jit(solution)/shard_map/ppermute | solution.py:192
  7.9 2.6 %collective-permute-start.5 = (f32[4,2304]{1,0:T(4,128)}, f32[4,2304]{1,0:T(4,128)S(1)}, u32[]{:S(2)}, u32[]{:S(2)}) collective-permute-start(f32[4,2304]{1,0:T(4,128)} %get-tuple-element.9), channel_id=1, source_target_pairs={{0,2},{1,3},{2,0},{3,1},{4,6},{5,7},{6,4},{7,5},{8,10},{9,11},{10,... | collective-permute-start | bytes 110600 | tf_op jit(solution)/shard_map/ppermute | solution.py:192
  10.5 0.0 collective-permute-done.3
  10.5 2.6 %collective-permute-start.4 = (f32[4,2304]{1,0:T(4,128)S(1)}, f32[4,2304]{1,0:T(4,128)S(1)}, u32[]{:S(2)}, u32[]{:S(2)}) collective-permute-start(f32[4,2304]{1,0:T(4,128)S(1)} %collective-permute-done.3), channel_id=1, source_target_pairs={{0,2},{1,3},{2,0},{3,1},{4,6},{5,7},{6,4},{7,5},{8,10},{9,11},{10,... | collective-permute-start | bytes 110600 | tf_op jit(solution)/shard_map/ppermute | solution.py:192
  13.1 0.0 collective-permute-start.1
  13.1 1.0 %collective-permute-done.5 = f32[4,2304]{1,0:T(4,128)S(1)} collective-permute-done((f32[4,2304]{1,0:T(4,128)}, f32[4,2304]{1,0:T(4,128)S(1)}, u32[]{:S(2)}, u32[]{:S(2)}) %collective-permute-start.5) | collective-permute-done | bytes 36896 | tf_op jit(solution)/shard_map/ppermute | solution.py:192
  14.1 0.0 collective-permute-start.10
  14.1 0.0 collective-permute-done.refs_1_
  14.1 0.0 copy-start
  14.1 0.5 %collective-permute-start.2 = (bf16[24,48,128]{2,1,0:T(8,128)(2,1)S(1)}, bf16[24,48,128]{2,1,0:T(8,128)(2,1)S(1)}, u32[]{:S(2)}, u32[]{:S(2)}) collective-permute-start(bf16[24,48,128]{2,1,0:T(8,128)(2,1)S(1)} %collective-permute-done.refs_1_), channel_id=1, source_target_pairs={{0,4},{4,0},{8,12},{12,8},{1,5},{5,1},{9,13},{13,9},{2,6},{6,2},{1... | collective-permute-start | bytes 884744 | tf_op jit(solution)/shard_map/ppermute | solution.py:182
  14.6 4.7 %collective-permute-done.9.refs_1_ = bf16[24,48,128]{2,1,0:T(8,128)(2,1)S(1)} collective-permute-done((bf16[24,48,128]{2,1,0:T(8,128)(2,1)}, bf16[24,48,128]{2,1,0:T(8,128)(2,1)S(1)}, u32[]{:S(2)}, u32[]{:S(2)}) %collective-permute-start.9) | collective-permute-done | bytes 294944 | tf_op jit(solution)/shard_map/ppermute | solution.py:182
  19.4 0.0 copy-start.1
  19.4 0.0 collective-permute-start.11
  19.4 0.0 collective-permute-done.4
  19.4 0.9 %select_select_fusion.3 = (f32[4,2304]{1,0:T(4,128)S(1)}, f32[4,2304]{1,0:T(4,128)S(1)}, f32[4,2304]{1,0:T(4,128)S(1)}, f32[4,2304]{1,0:T(4,128)S(1)}) fusion(f32[4,2304]{1,0:T(4,128)S(1)} %collective-permute-done.4, f32[4,2304]{1,0:T(4,128)S(1)} %collective-permute-done.5, f32[4,2304]{1,0:T(4,128)S(1)} %collective-permute-done.3, ...), kind=kLoop, calls=%fused_computation.4 | loop fusion | flops 110592 | bytes 294915 | tf_op jit(solution)/shard_map/jit(_where)/select_n | solution.py:198
  20.2 0.5 %collective-permute-start.7 = (f32[4,2304]{1,0:T(4,128)S(1)}, f32[4,2304]{1,0:T(4,128)S(1)}, u32[]{:S(2)}, u32[]{:S(2)}) collective-permute-start(f32[4,2304]{1,0:T(4,128)S(1)} %get-tuple-element.13), channel_id=1, source_target_pairs={{0,4},{4,0},{8,12},{12,8},{1,5},{5,1},{9,13},{13,9},{2,6},{6,2},{1... | collective-permute-start | bytes 110600 | tf_op jit(solution)/shard_map/ppermute | solution.py:200
  20.7 0.9 %collective-permute-done.7 = f32[4,2304]{1,0:T(4,128)S(1)} collective-permute-done((f32[4,2304]{1,0:T(4,128)S(1)}, f32[4,2304]{1,0:T(4,128)S(1)}, u32[]{:S(2)}, u32[]{:S(2)}) %collective-permute-start.7) | collective-permute-done | bytes 36896 | tf_op jit(solution)/shard_map/ppermute | solution.py:200
  21.6 1.7 %collective-permute-start.6 = (f32[4,2304]{1,0:T(4,128)S(1)}, f32[4,2304]{1,0:T(4,128)S(1)}, u32[]{:S(2)}, u32[]{:S(2)}) collective-permute-start(f32[4,2304]{1,0:T(4,128)S(1)} %get-tuple-element.14), channel_id=1, source_target_pairs={{0,8},{4,12},{8,0},{12,4},{1,9},{5,13},{9,1},{13,5},{2,10},{6,14},... | collective-permute-start | bytes 110600 | tf_op jit(solution)/shard_map/ppermute | solution.py:200
  23.4 2.2 %collective-permute-done.6 = f32[4,2304]{1,0:T(4,128)S(1)} collective-permute-done((f32[4,2304]{1,0:T(4,128)S(1)}, f32[4,2304]{1,0:T(4,128)S(1)}, u32[]{:S(2)}, u32[]{:S(2)}) %collective-permute-start.6) | collective-permute-done | bytes 36896 | tf_op jit(solution)/shard_map/ppermute | solution.py:200
  25.6 0.5 %collective-permute-start.8 = (f32[4,2304]{1,0:T(4,128)S(1)}, f32[4,2304]{1,0:T(4,128)S(1)}, u32[]{:S(2)}, u32[]{:S(2)}) collective-permute-start(f32[4,2304]{1,0:T(4,128)S(1)} %get-tuple-element.12), channel_id=1, source_target_pairs={{0,12},{4,8},{8,4},{12,0},{1,13},{5,9},{9,5},{13,1},{2,14},{6,10},... | collective-permute-start | bytes 110600 | tf_op jit(solution)/shard_map/ppermute | solution.py:200
  26.1 0.1 concatenate.12
  26.2 0.1 concatenate.13
  26.3 0.1 concatenate.14
  26.5 2.6 %collective-permute-done.8 = f32[4,2304]{1,0:T(4,128)S(1)} collective-permute-done((f32[4,2304]{1,0:T(4,128)S(1)}, f32[4,2304]{1,0:T(4,128)S(1)}, u32[]{:S(2)}, u32[]{:S(2)}) %collective-permute-start.8) | collective-permute-done | bytes 36896 | tf_op jit(solution)/shard_map/ppermute | solution.py:200
  29.1 0.1 concatenate.15
  29.2 0.9 %pad_maximum_fusion.refs_4_ = f32[192,192]{1,0:T(8,128)} fusion(f32[192,48]{1,0:T(8,128)S(1)} %concatenate.15, f32[192,48]{1,0:T(8,128)S(1)} %concatenate.14, f32[192,48]{1,0:T(8,128)S(1)} %concatenate.13, f32[192,48]{1,0:T(8,128)S(1)} %concatenate.12), kind=kLoop, calls=%fused_computation | loop fusion | flops 110592 | bytes 294912 | tf_op jit(solution)/shard_map/concatenate | solution.py:207
  30.1 0.0 collective-permute-done.10.refs_2_
  30.1 0.0 copy-start.4
  30.1 0.0 collective-permute-done.11.refs_3_
  30.1 0.0 copy-start.5
  30.1 0.0 copy-done.1
  30.1 0.7 %copy-done.4 = bf16[24,48,128]{2,1,0:T(8,128)(2,1)} copy-done((bf16[24,48,128]{2,1,0:T(8,128)(2,1)}, bf16[24,48,128]{2,1,0:T(8,128)(2,1)S(1)}, u32[]{:S(2)}) %copy-start.4) | copy-done | bytes 294936
  30.8 0.1 copy-done.5
  30.9 4.6 %attend.2.refs_11_ = f32[48,48,128]{2,1,0:T(8,128)} custom-call(bf16[24,48,128]{2,1,0:T(8,128)(2,1)} %get-tuple-element.10.refs_0_, bf16[24,48,128]{2,1,0:T(8,128)(2,1)} %copy-done.1, bf16[24,48,128]{2,1,0:T(8,128)(2,1)} %copy-done.4, bf16[24,48,128]{2,1,0:T(8,128)(2,1)} %copy-done.5, f32[192,192]{1,0:T(8,128)} %pad_maximum_fusion.refs_4_, ...), custom_call_target="tpu_custom_call" | custom-call | tf_op jit(solution)/shard_map/attend/pallas_call | solution.py:223
  35.5 0.0 copy-done
  35.6 0.0 collective-permute-done.1.refs_2_
  35.6 0.0 copy-start.2
  35.6 0.0 collective-permute-done.2.refs_3_
  35.6 0.7 %copy-done.2 = bf16[24,48,128]{2,1,0:T(8,128)(2,1)} copy-done((bf16[24,48,128]{2,1,0:T(8,128)(2,1)}, bf16[24,48,128]{2,1,0:T(8,128)(2,1)S(1)}, u32[]{:S(2)}) %copy-start.2) | copy-done | bytes 294936
  36.3 0.0 copy-start.3
  36.3 0.7 %copy-done.3 = bf16[24,48,128]{2,1,0:T(8,128)(2,1)} copy-done((bf16[24,48,128]{2,1,0:T(8,128)(2,1)}, bf16[24,48,128]{2,1,0:T(8,128)(2,1)S(1)}, u32[]{:S(2)}) %copy-start.3) | copy-done | bytes 294936
  37.0 4.7 %attend.3 = f32[48,48,128]{2,1,0:T(8,128)} custom-call(bf16[24,48,128]{2,1,0:T(8,128)(2,1)} %get-tuple-element.8.refs_0_, bf16[24,48,128]{2,1,0:T(8,128)(2,1)} %copy-done, bf16[24,48,128]{2,1,0:T(8,128)(2,1)} %copy-done.2, bf16[24,48,128]{2,1,0:T(8,128)(2,1)} %copy-done.3, f32[192,192]{1,0:T(8,128)} %pad_maximum_fusion.refs_4_, ...), custom_call_target="tpu_custom_call", output_to_operand_aliasing={{}: (11, {})} | custom-call | tf_op jit(solution)/shard_map/attend/pallas_call | solution.py:223
Async XLA Ops:
  2.9 11.3 %collective-permute-start = (bf16[24,48,128]{2,1,0:T(8,128)(2,1)}, bf16[24,48,128]{2,1,0:T(8,128)(2,1)S(1)}, u32[]{:S(2)}, u32[]{:S(2)}) collective-permute-start(bf16[24,48,128]{2,1,0:T(8,128)(2,1)} %get-tuple-element.8.refs_0_), channel_id=1, source_target_pairs={{0,8},{4,12},{8,0},{12,4},{1,9},{5,13},{9,1},{13,5},{2,10},{6,14},... | collective-permute-start | bytes 884744 | tf_op jit(solution)/shard_map/ppermute | solution.py:182
  5.8 13.5 %collective-permute-start.9 = (bf16[24,48,128]{2,1,0:T(8,128)(2,1)}, bf16[24,48,128]{2,1,0:T(8,128)(2,1)S(1)}, u32[]{:S(2)}, u32[]{:S(2)}) collective-permute-start(bf16[24,48,128]{2,1,0:T(8,128)(2,1)} %get-tuple-element.10.refs_0_), channel_id=1, source_target_pairs={{0,8},{4,12},{8,0},{12,4},{1,9},{5,13},{9,1},{13,5},{2,10},{6,14},... | collective-permute-start | bytes 884744 | tf_op jit(solution)/shard_map/ppermute | solution.py:182
  5.8 4.7 %collective-permute-start.3 = (f32[4,2304]{1,0:T(4,128)}, f32[4,2304]{1,0:T(4,128)S(1)}, u32[]{:S(2)}, u32[]{:S(2)}) collective-permute-start(f32[4,2304]{1,0:T(4,128)} %get-tuple-element.9), channel_id=1, source_target_pairs={{0,1},{1,0},{2,3},{3,2},{4,5},{5,4},{6,7},{7,6},{8,9},{9,8},{10,11... | collective-permute-start | bytes 110600 | tf_op jit(solution)/shard_map/ppermute | solution.py:192
  7.9 6.2 %collective-permute-start.5 = (f32[4,2304]{1,0:T(4,128)}, f32[4,2304]{1,0:T(4,128)S(1)}, u32[]{:S(2)}, u32[]{:S(2)}) collective-permute-start(f32[4,2304]{1,0:T(4,128)} %get-tuple-element.9), channel_id=1, source_target_pairs={{0,2},{1,3},{2,0},{3,1},{4,6},{5,7},{6,4},{7,5},{8,10},{9,11},{10,... | collective-permute-start | bytes 110600 | tf_op jit(solution)/shard_map/ppermute | solution.py:192
  10.5 8.8 %collective-permute-start.4 = (f32[4,2304]{1,0:T(4,128)S(1)}, f32[4,2304]{1,0:T(4,128)S(1)}, u32[]{:S(2)}, u32[]{:S(2)}) collective-permute-start(f32[4,2304]{1,0:T(4,128)S(1)} %collective-permute-done.3), channel_id=1, source_target_pairs={{0,2},{1,3},{2,0},{3,1},{4,6},{5,7},{6,4},{7,5},{8,10},{9,11},{10,... | collective-permute-start | bytes 110600 | tf_op jit(solution)/shard_map/ppermute | solution.py:192
  13.1 22.4 %collective-permute-start.1 = (bf16[24,48,128]{2,1,0:T(8,128)(2,1)}, bf16[24,48,128]{2,1,0:T(8,128)(2,1)S(1)}, u32[]{:S(2)}, u32[]{:S(2)}) collective-permute-start(bf16[24,48,128]{2,1,0:T(8,128)(2,1)} %get-tuple-element.8.refs_0_), channel_id=1, source_target_pairs={{0,4},{4,0},{8,12},{12,8},{1,5},{5,1},{9,13},{13,9},{2,6},{6,2},{1... | collective-permute-start | bytes 884744 | tf_op jit(solution)/shard_map/ppermute | solution.py:182
  14.1 15.9 %collective-permute-start.10 = (bf16[24,48,128]{2,1,0:T(8,128)(2,1)}, bf16[24,48,128]{2,1,0:T(8,128)(2,1)S(1)}, u32[]{:S(2)}, u32[]{:S(2)}) collective-permute-start(bf16[24,48,128]{2,1,0:T(8,128)(2,1)} %get-tuple-element.10.refs_0_), channel_id=1, source_target_pairs={{0,4},{4,0},{8,12},{12,8},{1,5},{5,1},{9,13},{13,9},{2,6},{6,2},{1... | collective-permute-start | bytes 884744 | tf_op jit(solution)/shard_map/ppermute | solution.py:182
  14.1 21.4 %copy-start = (bf16[24,48,128]{2,1,0:T(8,128)(2,1)}, bf16[24,48,128]{2,1,0:T(8,128)(2,1)S(1)}, u32[]{:S(2)}) copy-start(bf16[24,48,128]{2,1,0:T(8,128)(2,1)S(1)} %collective-permute-done.refs_1_) | copy-start | bytes 884740
  14.1 21.5 %collective-permute-start.2 = (bf16[24,48,128]{2,1,0:T(8,128)(2,1)S(1)}, bf16[24,48,128]{2,1,0:T(8,128)(2,1)S(1)}, u32[]{:S(2)}, u32[]{:S(2)}) collective-permute-start(bf16[24,48,128]{2,1,0:T(8,128)(2,1)S(1)} %collective-permute-done.refs_1_), channel_id=1, source_target_pairs={{0,4},{4,0},{8,12},{12,8},{1,5},{5,1},{9,13},{13,9},{2,6},{6,2},{1... | collective-permute-start | bytes 884744 | tf_op jit(solution)/shard_map/ppermute | solution.py:182
  19.4 10.7 %copy-start.1 = (bf16[24,48,128]{2,1,0:T(8,128)(2,1)}, bf16[24,48,128]{2,1,0:T(8,128)(2,1)S(1)}, u32[]{:S(2)}) copy-start(bf16[24,48,128]{2,1,0:T(8,128)(2,1)S(1)} %collective-permute-done.9.refs_1_) | copy-start | bytes 884740
  19.4 10.7 %collective-permute-start.11 = (bf16[24,48,128]{2,1,0:T(8,128)(2,1)S(1)}, bf16[24,48,128]{2,1,0:T(8,128)(2,1)S(1)}, u32[]{:S(2)}, u32[]{:S(2)}) collective-permute-start(bf16[24,48,128]{2,1,0:T(8,128)(2,1)S(1)} %collective-permute-done.9.refs_1_), channel_id=1, source_target_pairs={{0,4},{4,0},{8,12},{12,8},{1,5},{5,1},{9,13},{13,9},{2,6},{6,2},{1... | collective-permute-start | bytes 884744 | tf_op jit(solution)/shard_map/ppermute | solution.py:182
  20.2 1.4 %collective-permute-start.7 = (f32[4,2304]{1,0:T(4,128)S(1)}, f32[4,2304]{1,0:T(4,128)S(1)}, u32[]{:S(2)}, u32[]{:S(2)}) collective-permute-start(f32[4,2304]{1,0:T(4,128)S(1)} %get-tuple-element.13), channel_id=1, source_target_pairs={{0,4},{4,0},{8,12},{12,8},{1,5},{5,1},{9,13},{13,9},{2,6},{6,2},{1... | collective-permute-start | bytes 110600 | tf_op jit(solution)/shard_map/ppermute | solution.py:200
  21.6 4.0 %collective-permute-start.6 = (f32[4,2304]{1,0:T(4,128)S(1)}, f32[4,2304]{1,0:T(4,128)S(1)}, u32[]{:S(2)}, u32[]{:S(2)}) collective-permute-start(f32[4,2304]{1,0:T(4,128)S(1)} %get-tuple-element.14), channel_id=1, source_target_pairs={{0,8},{4,12},{8,0},{12,4},{1,9},{5,13},{9,1},{13,5},{2,10},{6,14},... | collective-permute-start | bytes 110600 | tf_op jit(solution)/shard_map/ppermute | solution.py:200
  25.6 3.5 %collective-permute-start.8 = (f32[4,2304]{1,0:T(4,128)S(1)}, f32[4,2304]{1,0:T(4,128)S(1)}, u32[]{:S(2)}, u32[]{:S(2)}) collective-permute-start(f32[4,2304]{1,0:T(4,128)S(1)} %get-tuple-element.12), channel_id=1, source_target_pairs={{0,12},{4,8},{8,4},{12,0},{1,13},{5,9},{9,5},{13,1},{2,14},{6,10},... | collective-permute-start | bytes 110600 | tf_op jit(solution)/shard_map/ppermute | solution.py:200
  30.1 0.7 %copy-start.4 = (bf16[24,48,128]{2,1,0:T(8,128)(2,1)}, bf16[24,48,128]{2,1,0:T(8,128)(2,1)S(1)}, u32[]{:S(2)}) copy-start(bf16[24,48,128]{2,1,0:T(8,128)(2,1)S(1)} %collective-permute-done.10.refs_2_) | copy-start | bytes 884740
  30.1 0.8 %copy-start.5 = (bf16[24,48,128]{2,1,0:T(8,128)(2,1)}, bf16[24,48,128]{2,1,0:T(8,128)(2,1)S(1)}, u32[]{:S(2)}) copy-start(bf16[24,48,128]{2,1,0:T(8,128)(2,1)S(1)} %collective-permute-done.11.refs_3_) | copy-start | bytes 884740
  35.6 0.7 %copy-start.2 = (bf16[24,48,128]{2,1,0:T(8,128)(2,1)}, bf16[24,48,128]{2,1,0:T(8,128)(2,1)S(1)}, u32[]{:S(2)}) copy-start(bf16[24,48,128]{2,1,0:T(8,128)(2,1)S(1)} %collective-permute-done.1.refs_2_) | copy-start | bytes 884740
  36.3 0.7 %copy-start.3 = (bf16[24,48,128]{2,1,0:T(8,128)(2,1)}, bf16[24,48,128]{2,1,0:T(8,128)(2,1)S(1)}, u32[]{:S(2)}) copy-start(bf16[24,48,128]{2,1,0:T(8,128)(2,1)S(1)} %collective-permute-done.2.refs_3_) | copy-start | bytes 884740
